TPU v7x, 256 devices: a whole 4x4x8 slice. The times are simulated.
256 devices in a mesh: ctx: 32 (over x, z_hi, y), exp: 8 (over z_lo, core).
Axes of the slice: x: 4, y: 4, z: 8 (z_hi: 2, z_lo: 4; z = z_hi * 4 + z_lo), core: 2. Of those that a mesh axis runs over, the one named last changes fastest.
Arguments:
- queries: bfloat16 [256, 32, 128], P(None, 'exp'), may hold values from -64 to 64
- keys: bfloat16 [32768, 8, 128], P('ctx', 'exp'), may hold values from -8 to 8
- values: bfloat16 [32768, 8, 128], P('ctx', 'exp'), may hold values from -32 to 32
- out_proj: bfloat16 [4096, 4096], P('exp', 'ctx'), may hold values from -0.09375 to 0.09375
- residual: bfloat16 [256, 4096], P('ctx'), may hold values from -6 to 6
- gain: float32 [4096], replicated, may hold values from 0.1 to 1.9
- routes: int32 [256, 2], P('ctx'), may hold values from 0 to 7, all different within a row; in each aligned block of 8 rows (0 to 7, 8 to 15, ...) at most 4 rows name the same one
- gates: float32 [256, 2], P('ctx'), may hold values from 0.25 to 1
- w_gate: bfloat16 [8, 4096, 14336], P('exp', None, 'ctx'), may hold values from -0.09375 to 0.09375
- w_up: bfloat16 [8, 4096, 14336], P('exp', None, 'ctx'), may hold values from -0.09375 to 0.09375
- w_down: bfloat16 [8, 14336, 4096], P('exp', 'ctx'), may hold values from -0.046875 to 0.046875
Outputs:
- mixed: bfloat16 [256, 4096], P('ctx', 'exp')
Inputs may be any that keep to these rules, and one draw needn't show every extreme that they name: `routes`: within each aligned block of 8 rows no expert is named by more than 4 rows, some expert is named by exactly 4 rows in some block, and the 2 experts of a row differ.
All inputs are finite; a program needn't handle non-finite values.
Results may differ from a plain program's by a relative error of at most 0.017.
Values may be sent and summed in bfloat16 or wider, within the bound.
A program may use at most 128 MiB of HBM per device.

v0:
```python
import math
import jax
import jax.numpy as jnp
from jax import lax
from jax.sharding import PartitionSpec as P


def joined(part, axis, combine):
    gathered = jax.tree.map(lambda a: lax.all_gather(a, axis), part)

    def take(source):
        return jax.tree.map(lambda a: lax.dynamic_index_in_dim(a, source, 0, False), gathered)

    return lax.fori_loop(
        1, lax.axis_size(axis), lambda source, state: combine(state, take(source)), take(0)
    )


def combine_parts(first_part, second_part):
    top_level = jnp.maximum(first_part[0], second_part[0])
    first_scale = jnp.exp(first_part[0] - top_level)
    second_scale = jnp.exp(second_part[0] - top_level)
    summed = first_part[1] * first_scale + second_part[1] * second_scale
    weighted = first_part[2] * first_scale[..., None] + second_part[2] * second_scale[..., None]
    return (top_level, summed, weighted)


def local(queries, keys, values, out_proj, residual, gain, routes, gates, w_gate, w_up, w_down):
    tokens_all, heads_local, head_dim = queries.shape
    key_rows, kv_local, unused_dim = keys.shape
    groups = heads_local // kv_local
    ctx_count = lax.axis_size("ctx")
    ctx_index = lax.axis_index("ctx")
    exp_index = lax.axis_index("exp")
    block_rows = residual.shape[0]
    total_len = key_rows * ctx_count
    score_scale = 1.0 / math.sqrt(head_dim)
    grouped = queries.reshape(tokens_all, kv_local, groups, head_dim)
    scores = (
        jnp.einsum("tgrd,sgd->gtrs", grouped, keys, preferred_element_type=jnp.float32)
        * score_scale
    )
    key_pos = ctx_index * key_rows + jnp.arange(key_rows, dtype=jnp.int32)
    query_pos = total_len - tokens_all + jnp.arange(tokens_all, dtype=jnp.int32)
    visible = (key_pos[None, :] <= query_pos[:, None])[None, :, None, :]
    scores = jnp.where(visible, scores, jnp.float32(-1e30))
    block_max = jnp.max(scores, axis=-1)
    expw = jnp.where(visible, jnp.exp(scores - block_max[..., None]), jnp.float32(0.0))
    block_sum = jnp.sum(expw, axis=-1)
    block_out = jnp.einsum(
        "gtrs,sgd->gtrd", expw.astype(jnp.bfloat16), values, preferred_element_type=jnp.float32
    )
    merged = joined((block_max, block_sum, block_out), "ctx", combine_parts)
    attended_all = merged[2] / merged[1][..., None]
    own_rows = lax.dynamic_slice_in_dim(attended_all, ctx_index * block_rows, block_rows, 1)
    attended = (
        own_rows.transpose(1, 0, 2, 3)
        .reshape(block_rows, heads_local * head_dim)
        .astype(jnp.bfloat16)
    )
    partial_value = jnp.dot(
        attended,
        lax.all_gather(out_proj, "ctx", axis=1, tiled=True),
        preferred_element_type=jnp.float32,
    )
    stream = residual.astype(jnp.float32) + lax.psum(
        partial_value.astype(jnp.bfloat16), "exp"
    ).astype(jnp.float32)
    normed = (
        stream * lax.rsqrt(jnp.mean(stream * stream, axis=-1, keepdims=True) + 1e-05) * gain
    ).astype(jnp.bfloat16)
    experts_local = w_gate.shape[0]
    expert_count = experts_local * lax.axis_size("exp")
    top_count = routes.shape[1]
    capacity = min(block_rows, 2 * top_count * block_rows // expert_count)
    flat_ids = routes.reshape(block_rows * top_count)
    onehot = (flat_ids[:, None] == jnp.arange(expert_count, dtype=jnp.int32)[None, :]).astype(
        jnp.int32
    )
    before = jnp.cumsum(onehot, axis=0, dtype=jnp.int32) - onehot
    slot_of = jnp.sum(before * onehot, axis=1, dtype=jnp.int32)
    mine_ids = exp_index * experts_local + jnp.arange(experts_local, dtype=jnp.int32)
    is_mine = flat_ids[:, None] == mine_ids[None, :]
    slot_hit = is_mine[:, :, None] & (
        slot_of[:, None, None] == jnp.arange(capacity, dtype=jnp.int32)[None, None, :]
    )
    slot_hit = slot_hit.astype(jnp.float32).reshape(block_rows, top_count, experts_local, capacity)
    dispatch_map = jnp.sum(slot_hit, axis=1)
    combine_map = jnp.sum(slot_hit * gates[:, :, None, None], axis=1)
    buffer = jnp.einsum(
        "tec,td->ced", dispatch_map.astype(jnp.bfloat16), normed, preferred_element_type=jnp.float32
    ).astype(jnp.bfloat16)
    shard_rows = lax.all_gather(buffer, "ctx", axis=0, tiled=True)
    gate_val = jnp.einsum("ned,edf->nef", shard_rows, w_gate, preferred_element_type=jnp.float32)
    up_val = jnp.einsum("ned,edf->nef", shard_rows, w_up, preferred_element_type=jnp.float32)
    act = (jax.nn.silu(gate_val) * up_val).astype(jnp.bfloat16)
    expert_out = lax.psum_scatter(
        jnp.einsum("nef,efd->ned", act, w_down, preferred_element_type=jnp.float32).astype(
            jnp.bfloat16
        ),
        "ctx",
        scatter_dimension=0,
        tiled=True,
    ).astype(jnp.float32)
    contribution = jnp.einsum(
        "tec,ced->td", combine_map, expert_out, precision=lax.Precision.HIGHEST
    )
    moe_share = lax.psum_scatter(
        contribution.astype(jnp.bfloat16), "exp", scatter_dimension=1, tiled=True
    ).astype(jnp.float32)
    feat_width = moe_share.shape[1]
    own_stream = lax.dynamic_slice_in_dim(stream, exp_index * feat_width, feat_width, 1)
    return (own_stream + moe_share).astype(jnp.bfloat16)


def solution(mesh):
    return jax.shard_map(
        local,
        mesh=mesh,
        in_specs=(
            P(None, "exp", None),
            P("ctx", "exp", None),
            P("ctx", "exp", None),
            P("exp", "ctx"),
            P("ctx", None),
            P(),
            P("ctx", None),
            P("ctx", None),
            P("exp", None, "ctx"),
            P("exp", None, "ctx"),
            P("exp", "ctx", None),
        ),
        out_specs=P("ctx", "exp"),
        check_vma=False,
    )
```

profile of v0, /device:TPU:2, one launch (start us, length us, event | category | flops | bytes accessed | tf_op | source)
XLA Modules:
  0.0 1042.4 jit_solution(11815722336202214809)
XLA Ops:
  7.5 2.0 fusion.8
  9.5 2.0 copy-done.1
  11.4 2.2 fusion.16
  14.5 3.7 fusion.15
  18.1 112.5 %all-gather = f32[8192,4]{0,1:T(4,128)S(1)} all-gather(f32[256,4]{0,1:T(4,128)S(1)} %get-tuple-element.241), channel_id=2, replica_groups=mesh['ctx'=32,'exp'=8] {'ctx'}, dimensions={0}, use_global_device_ids=true | all-gather | bytes 135168 | tf_op jit(solution)/shard_map/all_gather | solution.py:9
  130.7 123.6 %all-gather.1 = f32[8192,4]{0,1:T(4,128)S(1)} all-gather(f32[256,4]{0,1:T(4,128)S(1)} %fusion.15), channel_id=3, replica_groups=mesh['ctx'=32,'exp'=8] {'ctx'}, dimensions={0}, use_global_device_ids=true | all-gather | bytes 135168 | tf_op jit(solution)/shard_map/all_gather | solution.py:9
  254.9 12.9 %all-gather.11.cloned.1.call-done = f32[8192,4,128]{2,0,1:T(8,128)} async-done(((f32[256,4,128]{2,0,1:T(8,128)}), f32[8192,4,128]{2,0,1:T(8,128)}) %all-gather.11.cloned.1.call-update) | async-done | bytes 16777232 | tf_op jit(solution)/shard_map/all_gather | solution.py:9
  269.3 84.7 %while.19 = (s32[]{:T(128)}, f32[1,256,4]{1,2,0:T(4,128)S(1)}, f32[1,256,4]{1,2,0:T(4,128)S(1)}, f32[1,256,4,128]{3,2,1,0:T(4,128)S(1)}, f32[32,1,256,4]{2,3,1,0...) while((s32[]{:T(128)}, f32[1,256,4]{1,2,0:T(4,128)S(1)}, ...), condition=%wide.region_3.4_spmd, body=%wide.region_2.3_spmd.sunk | while | flops 400389 | bytes 2699419 | solution.py:14
  269.7 1.1 constant_dynamic-slice_fusion.3
  270.8 1.3 fusion.75
  272.4 1.1 constant_dynamic-slice_fusion.3
  273.5 1.3 fusion.75
  276.2 1.3 fusion.75
  277.9 1.1 constant_dynamic-slice_fusion.3
  279.0 1.3 fusion.75
  281.7 1.3 fusion.75
  283.3 1.1 constant_dynamic-slice_fusion.3
  284.4 1.3 fusion.75
  287.2 1.3 fusion.75
  288.8 1.1 constant_dynamic-slice_fusion.3
  289.9 1.3 fusion.75
  291.5 1.1 constant_dynamic-slice_fusion.3
  292.6 1.3 fusion.75
  295.4 1.3 fusion.75
  297.0 1.1 constant_dynamic-slice_fusion.3
  298.1 1.3 fusion.75
  300.8 1.3 fusion.75
  303.5 1.3 fusion.75
  305.2 1.1 constant_dynamic-slice_fusion.3
  306.3 1.3 fusion.75
  307.9 1.1 constant_dynamic-slice_fusion.3
  309.0 1.3 fusion.75
  311.7 1.3 fusion.75
  313.4 1.1 constant_dynamic-slice_fusion.3
  314.5 1.3 fusion.75
  317.2 1.3 fusion.75
  319.9 1.3 fusion.75
  321.6 1.1 constant_dynamic-slice_fusion.3
  322.7 1.3 fusion.75
  325.4 1.3 fusion.75
  327.0 1.1 constant_dynamic-slice_fusion.3
  328.1 1.3 fusion.75
  329.8 1.1 constant_dynamic-slice_fusion.3
  330.9 1.3 fusion.75
  332.5 1.1 constant_dynamic-slice_fusion.3
  333.6 1.3 fusion.75
  335.3 1.1 constant_dynamic-slice_fusion.3
  336.4 1.3 fusion.75
  339.1 1.3 fusion.75
  341.8 1.3 fusion.75
  344.5 1.3 fusion.75
  347.3 1.3 fusion.75
  350.0 1.3 fusion.75
  352.7 1.3 fusion.75
  354.3 45.0 %all-gather.7.cloned.1.call-done = bf16[512,4096]{1,0:T(8,128)(2,1)} async-done(((bf16[512,128]{1,0:T(8,128)(2,1)}), bf16[512,4096]{1,0:T(8,128)(2,1)}) %all-gather.7.cloned.1.call-update) | async-done | bytes 4194320 | tf_op jit(solution)/shard_map/all_gather | solution.py:63
  399.3 3.5 convolution_convert_fusion.2
  402.9 65.4 %all-reduce.4.cloned.1.call-done = bf16[8,4096]{1,0:T(8,128)(2,1)} async-done(((bf16[8,4096]{1,0:T(8,128)(2,1)}), bf16[8,4096]{1,0:T(8,128)(2,1)}) %all-reduce.4.cloned.1.call-update) | async-done | bytes 65552 | tf_op jit(solution)/shard_map/psum | solution.py:66
  471.1 90.5 %all-gather.9.cloned.1.call-done = bf16[128,1,4096]{2,1,0:T(2,128)(2,1)} async-done(((bf16[4,1,4096]{2,1,0:T(2,128)(2,1)}), bf16[128,1,4096]{2,1,0:T(2,128)(2,1)}) %all-gather.9.cloned.1.call-update) | async-done | bytes 1048592 | tf_op jit(solution)/shard_map/all_gather | solution.py:93
  561.6 4.8 fusion.19
  566.4 7.3 fusion.6
  574.9 405.6 %all-reduce.6.cloned.1.call-done = bf16[128,1,4096]{2,0,1:T(8,128)(2,1)} async-done(((bf16[128,1,4096]{2,0,1:T(8,128)(2,1)}), bf16[128,1,4096]{2,0,1:T(8,128)(2,1)}) %all-reduce.6.cloned.1.call-update) | async-done | bytes 1048592
  980.5 1.7 convolution_convert_fusion.1
  982.3 52.0 %reduce-scatter.3.cloned.1.call-done = bf16[8,512]{1,0:T(8,128)(2,1)} async-done(((bf16[8,4096]{1,0:T(8,128)(2,1)}), bf16[8,512]{1,0:T(8,128)(2,1)}) %reduce-scatter.3.cloned.1.call-update) | async-done | bytes 8208 | tf_op jit(solution)/shard_map/reduce_scatter | solution.py:108
  1034.3 1.3 add_convert_fusion
  (224 shorter events, 34.6 us)
Async XLA Ops:
  6.5 1.0 copy-start
  6.5 4.9 copy-start.7
  6.5 261.3 %all-gather.11.cloned.1.call-start = ((), (), s32[]{:S(2)}) async-start(), calls=%async_computation.5 | async-start | bytes 17301504 | tf_op jit(solution)/shard_map/all_gather | solution.py:9
  9.4 2.0 copy-start.1
  13.6 240.7 %copy-start.5 = (s32[8,2]{0,1:T(2,128)S(1)}, s32[8,2]{0,1:T(2,128)}, u32[]{:S(2)}) copy-start(s32[8,2]{0,1:T(2,128)} %param.19) | copy-start | bytes 196
  13.7 385.6 %all-gather.7.cloned.1.call-start = ((), (), s32[]{:S(2)}) async-start(), calls=%async_computation.1 | async-start | bytes 4325376 | tf_op jit(solution)/shard_map/all_gather | solution.py:63
  14.4 453.8 %all-reduce.4.cloned.1.call-start = ((), (), s32[]{:S(2)}) async-start(), calls=%async_computation.2 | async-start | bytes 131072 | tf_op jit(solution)/shard_map/psum | solution.py:66
  354.0 48.8 %copy-start.6 = (f32[8,2]{0,1:T(2,128)S(1)}, f32[8,2]{0,1:T(2,128)}, u32[]{:S(2)}) copy-start(f32[8,2]{0,1:T(2,128)} %param.20) | copy-start | bytes 196
  354.0 114.2 %copy-start.3 = (bf16[8,4096]{1,0:T(8,128)(2,1)S(1)}, bf16[8,4096]{1,0:T(8,128)(2,1)}, u32[]{:S(2)}) copy-start(bf16[8,4096]{1,0:T(8,128)(2,1)} %param.17) | copy-start | bytes 196612
  354.1 115.2 %copy-start.4 = (f32[4096]{0:T(1024)S(1)}, f32[4096]{0:T(1024)}, u32[]{:S(2)}) copy-start(f32[4096]{0:T(1024)} %param.18) | copy-start | bytes 49156
  402.8 158.8 %all-gather.9.cloned.1.call-start = ((), (), s32[]{:S(2)}) async-start(), calls=%async_computation.3 | async-start | bytes 2162688 | tf_op jit(solution)/shard_map/all_gather | solution.py:93
  471.0 509.5 %all-reduce.6.cloned.1.call-start = ((), (), s32[]{:S(2)}) async-start(), calls=%async_computation.6 | async-start | bytes 2097152
  561.6 4.8 copy-start.2
  566.3 7.4 copy-start.8
  573.6 460.6 %reduce-scatter.3.cloned.1.call-start = ((), (), s32[]{:S(2)}) async-start(), calls=%async_computation.4 | async-start | bytes 73728 | tf_op jit(solution)/shard_map/reduce_scatter | solution.py:108
Sparse Core Ops, SparseCore 0:
  13.8 254.0 all-gather.10
  271.1 128.1 all-gather.6
  402.9 65.3 all-reduce.3
  472.2 89.3 all-gather.8
  573.8 406.6 all-reduce.5
  982.9 51.3 reduce-scatter.2
where the time goes:
time: 1040 us
  waiting for transfers between devices  672 us (65%)
  blocking collectives  236 us (23%)
  local copies, waits for them, and re-layouts  48.1 us (5%)
  other arithmetic  47.1 us (5%)
  matrix products  22.4 us (2%)
  between operations  14.3 us (1%)
    unnamed x7, waiting for transfers between devices  406 us
    all_gather x2, blocking collectives, joined(): gathered = jax.tree.map(lambda a: lax.all_gather(a, axis), part)  236 us
    all_gather x1, waiting for transfers between devices, local(): shard_rows = lax.all_gather(buffer, 'ctx', axis=0, tiled=True)  90.5 us
    psum x1, waiting for transfers between devices, local(): lax.psum(partial_value.astype(jnp.bfloat16), 'exp').astype(jnp.float32)  65.4 us
    reduce_scatter x1, waiting for transfers between devices, local(): lax.psum_scatter(contribution.astype(jnp.bfloat16), 'exp', scatter_dimens...  52 us
    all_gather x1, waiting for transfers between devices, local(): lax.all_gather(out_proj, 'ctx', axis=1, tiled=True)  45 us
    add x31, other arithmetic, combine_parts(): first_part[2] * first_scale[..., None]  39.3 us
    dynamic_slice x31, local copies, waits for them, and re-layouts, take(): lax.dynamic_index_in_dim(a, source, 0, False)  33.8 us
  transfers between devices with their start and end apart: 6, of which 6 were waited for; matrix products, arithmetic and copies ran while one was open for 9% of the time, Pallas kernels for 0%

commit v1 on v0

--- a/solution.py
+++ b/solution.py
@@ -60,7 +60,9 @@
     )
     partial_value = jnp.dot(
         attended,
-        lax.all_gather(out_proj, "ctx", axis=1, tiled=True),
+        jnp.concatenate(
+            lax.all_to_all(jnp.stack([out_proj] * lax.axis_size("ctx")), "ctx", 0, 0), axis=1
+        ),
         preferred_element_type=jnp.float32,
     )
     stream = residual.astype(jnp.float32) + lax.psum(

time: 1040 us -> 1120 us (1.077)
  blocking collectives: 236 us -> 328 us
  waiting for transfers between devices: 672 us -> 636 us
  starting transfers between devices: 0.21 us -> 14.8 us
    all_gather x2, blocking collectives: 236 us -> 328 us  [joined(): gathered = jax.tree.map(lambda a: lax.all_gather(a, axis), part)]
    all_gather x1 -> x0, waiting for transfers between devices: 45 us -> none  [local(): lax.all_gather(out_proj, 'ctx', axis=1, tiled=True)]
    psum x1, waiting for transfers between devices: 65.4 us -> 88.1 us  [local(): lax.psum(partial_value.astype(jnp.bfloat16), 'exp').astype(jnp.float32)]
    all_to_all x0 -> x1, starting transfers between devices: none -> 14.4 us  [local(): lax.all_to_all(jnp.stack([out_proj] * lax.axis_size('ctx')), 'ctx', 0, 0)]
    all_gather x1, waiting for transfers between devices: 12.9 us -> 0.02 us  [joined(): gathered = jax.tree.map(lambda a: lax.all_gather(a, axis), part)]
    unnamed x7 -> x6, waiting for transfers between devices: 406 us -> 406 us
  transfers between devices with their start and end apart: 6 -> 6, of which waited for: 6 -> 4; matrix products, arithmetic and copies ran while one was open for 9% -> 8% of each run, Pallas kernels for 0% -> 0%
where the time goes in v1:
time: 1120 us
  waiting for transfers between devices  636 us (57%)
  blocking collectives  328 us (29%)
  local copies, waits for them, and re-layouts  50.6 us (5%)
  other arithmetic  47.1 us (4%)
  matrix products  22.9 us (2%)
  starting transfers between devices  14.8 us (1%)
  between operations  14 us (1%)
    unnamed x6, waiting for transfers between devices  406 us
    all_gather x2, blocking collectives, joined(): gathered = jax.tree.map(lambda a: lax.all_gather(a, axis), part)  328 us
    all_gather x1, waiting for transfers between devices, local(): shard_rows = lax.all_gather(buffer, 'ctx', axis=0, tiled=True)  90.5 us
    psum x1, waiting for transfers between devices, local(): lax.psum(partial_value.astype(jnp.bfloat16), 'exp').astype(jnp.float32)  88.1 us
    reduce_scatter x1, waiting for transfers between devices, local(): lax.psum_scatter(contribution.astype(jnp.bfloat16), 'exp', scatter_dimens...  52 us
    add x31, other arithmetic, combine_parts(): first_part[2] * first_scale[..., None]  39.3 us
    dynamic_slice x31, local copies, waits for them, and re-layouts, take(): lax.dynamic_index_in_dim(a, source, 0, False)  33.7 us
  transfers between devices with their start and end apart: 6, of which 4 were waited for; matrix products, arithmetic and copies ran while one was open for 8% of the time, Pallas kernels for 0%

profile of v1, /device:TPU:2, one launch (start us, length us, event | category | flops | bytes accessed | tf_op | source)
XLA Modules:
  0.0 1115.4 jit_solution(8581246615379384005)
XLA Ops:
  7.5 2.0 fusion.8
  9.5 1.9 copy-done.1
  11.4 2.2 fusion.16
  13.8 2.4 stack.2
  16.2 14.4 %all-to-all-start = ((bf16[32,512,128]{1,2,0:T(8,128)(2,1)}), bf16[32,512,128]{1,2,0:T(8,128)(2,1)}, u32[]{:S(2)}, u32[]{:S(2)}) async-start(bf16[32,512,128]{1,2,0:T(8,128)(2,1)} %stack.2), calls=%async_computation | async-start | bytes 8388608 | tf_op jit(solution)/shard_map/all_to_all | solution.py:64
  31.3 213.7 %all-gather = f32[8192,4]{0,1:T(4,128)S(1)} all-gather(f32[256,4]{0,1:T(4,128)S(1)} %get-tuple-element.241), channel_id=2, replica_groups=mesh['ctx'=32,'exp'=8] {'ctx'}, dimensions={0}, use_global_device_ids=true | all-gather | bytes 135168 | tf_op jit(solution)/shard_map/all_gather | solution.py:9
  245.0 3.7 fusion.15
  248.7 113.9 %all-gather.1 = f32[8192,4]{0,1:T(4,128)S(1)} all-gather(f32[256,4]{0,1:T(4,128)S(1)} %fusion.15), channel_id=3, replica_groups=mesh['ctx'=32,'exp'=8] {'ctx'}, dimensions={0}, use_global_device_ids=true | all-gather | bytes 135168 | tf_op jit(solution)/shard_map/all_gather | solution.py:9
  364.1 84.7 %while.19 = (s32[]{:T(128)}, f32[1,256,4]{1,2,0:T(4,128)S(1)}, f32[1,256,4]{1,2,0:T(4,128)S(1)}, f32[1,256,4,128]{3,2,1,0:T(4,128)S(1)}, f32[32,1,256,4]{2,3,1,0...) while((s32[]{:T(128)}, f32[1,256,4]{1,2,0:T(4,128)S(1)}, ...), condition=%wide.region_3.4_spmd, body=%wide.region_2.3_spmd.sunk | while | flops 400389 | bytes 2699419 | solution.py:14
  364.5 1.1 constant_dynamic-slice_fusion.3
  365.5 1.3 fusion.75
  367.2 1.1 constant_dynamic-slice_fusion.3
  368.3 1.3 fusion.75
  369.9 1.1 constant_dynamic-slice_fusion.3
  371.0 1.3 fusion.75
  372.6 1.1 constant_dynamic-slice_fusion.3
  373.7 1.3 fusion.75
  375.4 1.1 constant_dynamic-slice_fusion.3
  376.5 1.3 fusion.75
  379.2 1.3 fusion.75
  381.9 1.3 fusion.75
  383.6 1.1 constant_dynamic-slice_fusion.3
  384.7 1.3 fusion.75
  387.4 1.3 fusion.75
  390.1 1.3 fusion.75
  391.8 1.1 constant_dynamic-slice_fusion.3
  392.9 1.3 fusion.75
  395.6 1.3 fusion.75
  397.2 1.1 constant_dynamic-slice_fusion.3
  398.3 1.3 fusion.75
  400.0 1.1 constant_dynamic-slice_fusion.3
  401.0 1.3 fusion.75
  403.8 1.3 fusion.75
  405.4 1.1 constant_dynamic-slice_fusion.3
  406.5 1.3 fusion.75
  409.2 1.3 fusion.75
  412.0 1.3 fusion.75
  413.6 1.1 constant_dynamic-slice_fusion.3
  414.7 1.3 fusion.75
  417.4 1.3 fusion.75
  420.2 1.3 fusion.75
  421.8 1.1 constant_dynamic-slice_fusion.3
  422.9 1.3 fusion.75
  425.6 1.3 fusion.75
  427.3 1.1 constant_dynamic-slice_fusion.3
  428.4 1.3 fusion.75
  431.1 1.3 fusion.75
  433.8 1.3 fusion.75
  435.5 1.1 constant_dynamic-slice_fusion.3
  436.6 1.3 fusion.75
  439.3 1.3 fusion.75
  442.0 1.3 fusion.75
  443.7 1.1 constant_dynamic-slice_fusion.3
  444.7 1.3 fusion.75
  447.5 1.3 fusion.75
  449.1 4.0 convolution_convert_fusion.2
  453.2 88.1 %all-reduce.4.cloned.1.call-done = bf16[8,4096]{1,0:T(8,128)(2,1)} async-done(((bf16[8,4096]{1,0:T(8,128)(2,1)}), bf16[8,4096]{1,0:T(8,128)(2,1)}) %all-reduce.4.cloned.1.call-update) | async-done | bytes 65552 | tf_op jit(solution)/shard_map/psum | solution.py:68
  544.2 90.5 %all-gather.6.cloned.1.call-done = bf16[128,1,4096]{2,1,0:T(2,128)(2,1)} async-done(((bf16[4,1,4096]{2,1,0:T(2,128)(2,1)}), bf16[128,1,4096]{2,1,0:T(2,128)(2,1)}) %all-gather.6.cloned.1.call-update) | async-done | bytes 1048592 | tf_op jit(solution)/shard_map/all_gather | solution.py:95
  634.7 4.8 fusion.19
  639.5 7.3 fusion.6
  648.1 405.7 %all-reduce.6.cloned.1.call-done = bf16[128,1,4096]{2,0,1:T(8,128)(2,1)} async-done(((bf16[128,1,4096]{2,0,1:T(8,128)(2,1)}), bf16[128,1,4096]{2,0,1:T(8,128)(2,1)}) %all-reduce.6.cloned.1.call-update) | async-done | bytes 1048592
  1053.8 1.7 convolution_convert_fusion.1
  1055.5 52.0 %reduce-scatter.3.cloned.1.call-done = bf16[8,512]{1,0:T(8,128)(2,1)} async-done(((bf16[8,4096]{1,0:T(8,128)(2,1)}), bf16[8,512]{1,0:T(8,128)(2,1)}) %reduce-scatter.3.cloned.1.call-update) | async-done | bytes 8208 | tf_op jit(solution)/shard_map/reduce_scatter | solution.py:110
  1107.5 1.3 add_convert_fusion
  (227 shorter events, 34.2 us)
Async XLA Ops:
  6.5 1.0 copy-start
  6.5 4.9 copy-start.8
  6.5 356.1 %all-gather.8.cloned.1.call-start = ((), (), s32[]{:S(2)}) async-start(), calls=%async_computation.5 | async-start | bytes 17301504 | tf_op jit(solution)/shard_map/all_gather | solution.py:9
  9.4 2.0 copy-start.1
  11.4 2.2 copy-start.4
  16.2 14.5 %copy-start.6 = (s32[8,2]{0,1:T(2,128)S(1)}, s32[8,2]{0,1:T(2,128)}, u32[]{:S(2)}) copy-start(s32[8,2]{0,1:T(2,128)} %param.19) | copy-start | bytes 196
  16.2 432.9 %all-to-all-start = ((bf16[32,512,128]{1,2,0:T(8,128)(2,1)}), bf16[32,512,128]{1,2,0:T(8,128)(2,1)}, u32[]{:S(2)}, u32[]{:S(2)}) async-start(bf16[32,512,128]{1,2,0:T(8,128)(2,1)} %stack.2), calls=%async_computation | async-start | bytes 8388608 | tf_op jit(solution)/shard_map/all_to_all | solution.py:64
  30.6 510.6 %all-reduce.4.cloned.1.call-start = ((), (), s32[]{:S(2)}) async-start(), calls=%async_computation.2 | async-start | bytes 131072 | tf_op jit(solution)/shard_map/psum | solution.py:68
  448.8 4.4 copy-start.7
  448.8 92.5 %copy-start.3 = (bf16[8,4096]{1,0:T(8,128)(2,1)S(1)}, bf16[8,4096]{1,0:T(8,128)(2,1)}, u32[]{:S(2)}) copy-start(bf16[8,4096]{1,0:T(8,128)(2,1)} %param.17) | copy-start | bytes 196612
  448.8 93.5 %copy-start.5 = (f32[4096]{0:T(1024)S(1)}, f32[4096]{0:T(1024)}, u32[]{:S(2)}) copy-start(f32[4096]{0:T(1024)} %param.18) | copy-start | bytes 49156
  453.1 181.6 %all-gather.6.cloned.1.call-start = ((), (), s32[]{:S(2)}) async-start(), calls=%async_computation.3 | async-start | bytes 2162688 | tf_op jit(solution)/shard_map/all_gather | solution.py:95
  544.0 509.8 %all-reduce.6.cloned.1.call-start = ((), (), s32[]{:S(2)}) async-start(), calls=%async_computation.6 | async-start | bytes 2097152
  634.7 4.8 copy-start.2
  639.5 7.4 copy-start.9
  646.8 460.8 %reduce-scatter.3.cloned.1.call-start = ((), (), s32[]{:S(2)}) async-start(), calls=%async_computation.4 | async-start | bytes 73728 | tf_op jit(solution)/shard_map/reduce_scatter | solution.py:110
Sparse Core Ops, SparseCore 0:
  13.7 327.7 all-gather.7
  453.2 87.9 all-reduce.3
  545.3 89.3 all-gather.5
  646.9 406.8 all-reduce.5
  1056.1 51.3 reduce-scatter.2
